TPU v7x, 32 devices: a whole 2x2x4 slice. The times are simulated.
32 devices in a mesh: box: 8 (over z, x), path: 4 (over y, core).
Axes of the slice: x: 2, y: 2, z: 4, core: 2. Of those that a mesh axis runs over, the one named last changes fastest.
Arguments:
- features: float32 [1024, 9, 128], P('box'), may hold values from -6 to 6
- positions: float32 [3, 1024], P(None, 'box'), may hold values from 0 to 96, as said below
- cotangent: bfloat16 [1024, 9, 128], P('box'), may hold values from -6 to 6
- weights: float32 [8, 8, 128], P('path'), may hold values from -2 to 2
- neighbours: int32 [16, 3], P('box'), may hold values from 0 to 3, as said below
- send_list: int32 [8, 2], P('box'), may hold values from 0 to 1, as said below
Outputs:
- grad_features: float32 [1024, 9, 128], P(('box', 'path'))
- grad_weights: float32 [8, 8, 128], P('path')
Inputs may be any that keep to these rules, and one draw needn't show every extreme that they name: `positions`: stored block s of box b has a place g = b * 2 + (a permutation of 0 to 1 within the box) along a chain; its atoms lie near the points of a grid of spacing 1.5 with 4 x 4 points across and 4 along the third coordinate, the first coordinate between 6 g and 6 g + 6, each moved by at most 0.35 in each coordinate. Blocks whose places differ by two or more have no atoms within 5 of each other. `neighbours`: row g lists the block itself (its stored index), the block one place before it and the block one place after it along the chain, as table indices: below 2 the box's own stored blocks, 2 the block received from the previous box (its last block along the chain), 3 the block received from the next box (its first block along the chain). The relation is symmetric. send_list[b, 0] is the stored index of the first block of box b's stretch of the chain and send_list[b, 1] that of the last.
All inputs are finite; a program needn't handle non-finite values.
Results may differ from a plain program's by a relative error of at most 0.0045.
Values may be sent and summed in bfloat16 or wider, within the bound.
A program may use at most 64 MiB of HBM per device.

v0:
```python
import math
import jax
import jax.numpy as jnp
from jax import lax
from jax.sharding import PartitionSpec as P

BASIS = 8
BLOCK = 64
NEIGHBOURS = 3
PATHS = 8
cutoff_radius = 5.0
edge_scale = 0.2
basis_width = 0.8
root_three = math.sqrt(3.0)
path_terms = [
    [(0, [(0, 0, 1.0)])],
    [(0, [(1, 1, 1.0), (2, 2, 1.0), (3, 3, 1.0)])],
    [(1, [(1, 0, 1.0)]), (2, [(2, 0, 1.0)]), (3, [(3, 0, 1.0)])],
    [(1, [(0, 1, 1.0)]), (2, [(0, 2, 1.0)]), (3, [(0, 3, 1.0)])],
    [
        (4, [(4, 0, 1.0)]),
        (5, [(5, 0, 1.0)]),
        (6, [(6, 0, 1.0)]),
        (7, [(7, 0, 1.0)]),
        (8, [(8, 0, 1.0)]),
    ],
    [
        (4, [(0, 4, 1.0)]),
        (5, [(0, 5, 1.0)]),
        (6, [(0, 6, 1.0)]),
        (7, [(0, 7, 1.0)]),
        (8, [(0, 8, 1.0)]),
    ],
    [
        (1, [(3, 2, 1.0), (2, 3, -1.0)]),
        (2, [(1, 3, 1.0), (3, 1, -1.0)]),
        (3, [(2, 1, 1.0), (1, 2, -1.0)]),
    ],
    [(0, [(4, 4, 1.0), (5, 5, 1.0), (6, 6, 1.0), (7, 7, 1.0), (8, 8, 1.0)])],
]


def with_halo(cells, sides, width):
    for axis, dim in sides:
        count = lax.axis_size(axis)
        ends = count - 1
        head = lax.slice_in_dim(cells, 0, width, axis=dim)
        tail = lax.slice_in_dim(cells, cells.shape[dim] - width, cells.shape[dim], axis=dim)
        cells = jnp.concatenate(
            [
                lax.ppermute(tail, axis, [(i, (i + 1) % count) for i in range(ends)]),
                cells,
                lax.ppermute(head, axis, [((i + 1) % count, i) for i in range(ends)]),
            ],
            axis=dim,
        )
    return cells


def edge_tensor(anchor, target):
    offset = target[:, None, :] - anchor[:, :, None]
    square = jnp.sum(offset * offset, axis=0)
    inside = square > 0.01
    distance = jnp.sqrt(jnp.where(inside, square, 1.0))
    direction = offset / distance[None]
    envelope = jnp.where(
        inside & (distance < cutoff_radius),
        0.5 * (jnp.cos(math.pi * distance / cutoff_radius) + 1.0),
        0.0,
    )
    centres = (jnp.arange(BASIS, dtype=jnp.float32) + 0.5) * (cutoff_radius / BASIS)
    radial = (
        jnp.exp(-jnp.square((distance[None] - centres[:, None, None]) / basis_width))
        * (edge_scale * envelope)[None]
    )
    eastward = direction[0]
    northward = direction[1]
    upward = direction[2]
    harmonics = jnp.stack(
        [
            jnp.ones_like(eastward),
            eastward,
            northward,
            upward,
            root_three * eastward * northward,
            root_three * northward * upward,
            0.5 * (3.0 * upward * upward - 1.0),
            root_three * eastward * upward,
            0.5 * root_three * (eastward * eastward - northward * northward),
        ]
    )
    return (harmonics[:, None] * radial[None]).astype(jnp.bfloat16)


def forward_terms(paths, weights, edge_table, rounded):
    source_rows = rounded.shape[0]
    target_rows = edge_table.shape[2]
    channels = rounded.shape[2]
    outputs = [jnp.zeros((target_rows, channels), jnp.float32) for output in range(9)]
    for weight_slot, path_number in enumerate(paths):
        for output, term_list in path_terms[path_number]:
            pieces = []
            stacked = []
            for harmonic, source, factor in term_list:
                signed = edge_table[harmonic] if factor > 0 else -edge_table[harmonic]
                pieces.append(signed.reshape(BASIS * target_rows, source_rows))
                stacked.append(rounded[:, source, :])
            product = jnp.dot(
                jnp.concatenate(pieces, axis=1),
                jnp.concatenate(stacked, axis=0),
                preferred_element_type=jnp.float32,
            )
            product = product.reshape(BASIS, target_rows, channels)
            outputs[output] = outputs[output] + jnp.sum(
                weights[weight_slot][:, None, :] * product, axis=0
            )
    return jnp.stack(outputs, axis=1)


def transpose_terms(paths, weights, edge_table, cotangent_rows, source_features):
    rows = source_features.shape[0]
    channels = source_features.shape[2]
    outputs = [jnp.zeros((rows, channels), jnp.float32) for output in range(9)]
    weight_parts = []
    for weight_slot, path_number in enumerate(paths):
        weight_part = jnp.zeros((BASIS, channels), jnp.float32)
        for output, term_list in path_terms[path_number]:
            for harmonic, source, factor in term_list:
                gathered = lax.dot_general(
                    edge_table[harmonic],
                    cotangent_rows[:, output, :],
                    (((1,), (0,)), ((), ())),
                    preferred_element_type=jnp.float32,
                )
                outputs[source] = outputs[source] + factor * jnp.sum(
                    weights[weight_slot][:, None, :] * gathered, axis=0
                )
                weight_part = weight_part + factor * jnp.sum(
                    source_features[:, source, :][None] * gathered, axis=1
                )
        weight_parts.append(weight_part)
    return (jnp.stack(outputs, axis=1), jnp.stack(weight_parts, axis=0))


def gate_back(message, cotangent):
    incoming = cotangent.astype(jnp.float32)
    scalar = message[:, 0]
    sigma = jax.nn.sigmoid(scalar)
    slope = sigma * (1.0 + scalar * (1.0 - sigma))
    coupling = jnp.sum(incoming[:, 1:] * message[:, 1:], axis=1)
    leading = incoming[:, 0] * slope + sigma * (1.0 - sigma) * coupling
    others = incoming[:, 1:] * sigma[:, None]
    return jnp.concatenate([leading[:, None], others], axis=1).astype(jnp.bfloat16)


def on_device(features, positions, cotangent, weights, neighbours, send_list):
    local_blocks = neighbours.shape[0]
    local_rows = features.shape[0]
    channels = features.shape[2]
    block_features = features.reshape(local_blocks, BLOCK, 9, channels)
    block_places = positions.reshape(3, local_blocks, BLOCK).transpose(1, 0, 2)
    outgoing = send_list[0]
    padded_features, padded_places = (
        with_halo(block_features[outgoing], (("box", 0),), 1),
        with_halo(block_places[outgoing], (("box", 0),), 1),
    )
    table_features = jnp.concatenate(
        [block_features, padded_features[:1], padded_features[3:]], axis=0
    )
    table_places = jnp.concatenate([block_places, padded_places[:1], padded_places[3:]], axis=0)
    table_rounded = table_features.astype(jnp.bfloat16)
    group = lax.axis_index("path")
    share_rows = local_rows // lax.axis_size("path")
    cotangent_share = lax.dynamic_slice_in_dim(cotangent, group * share_rows, share_rows, 0)
    all_weights = lax.all_gather(weights, "path", axis=0, tiled=True)
    all_paths = list(range(PATHS))
    slab_rows = math.gcd(share_rows, BLOCK)
    slab_numbers = jnp.arange(share_rows // slab_rows, dtype=jnp.int32)

    def slab_anchor(slab_index):
        first_row = group * share_rows + slab_index * slab_rows
        block_number = first_row // BLOCK
        within_row = first_row % BLOCK
        anchor_rows = lax.dynamic_slice_in_dim(block_places[block_number], within_row, slab_rows, 1)
        return (block_number, within_row, anchor_rows)

    def forward_slab(slab_index):
        block_number, within_row, anchor_rows = slab_anchor(slab_index)
        total = jnp.zeros((slab_rows, 9, channels), jnp.float32)
        for neighbour in range(NEIGHBOURS):
            table_slot = neighbours[block_number, neighbour]
            edge_table = edge_tensor(anchor_rows, table_places[table_slot])
            total = total + forward_terms(
                all_paths, all_weights, edge_table, table_rounded[table_slot]
            )
        return total

    message_rows = lax.map(forward_slab, slab_numbers).reshape(share_rows, 9, channels)
    gate_rows = gate_back(message_rows, cotangent_share)
    message_cotangent = lax.all_gather(gate_rows, "path", axis=0, tiled=True)
    cotangent_blocks = message_cotangent.reshape(local_blocks, BLOCK, 9, channels)
    padded_gate = with_halo(cotangent_blocks[outgoing], (("box", 0),), 1)
    table_gate = jnp.concatenate([cotangent_blocks, padded_gate[:1], padded_gate[3:]], axis=0)

    def pull_slab(slab_index):
        block_number, within_row, anchor_rows = slab_anchor(slab_index)
        own_features = lax.dynamic_slice_in_dim(
            block_features[block_number], within_row, slab_rows, 0
        )
        total = jnp.zeros((slab_rows, 9, channels), jnp.float32)
        weight_total = jnp.zeros((PATHS, BASIS, channels), jnp.float32)
        for neighbour in range(NEIGHBOURS):
            table_slot = neighbours[block_number, neighbour]
            edge_table = edge_tensor(table_places[table_slot], anchor_rows)
            contribution, weight_part = transpose_terms(
                all_paths, all_weights, edge_table, table_gate[table_slot], own_features
            )
            total = total + contribution
            weight_total = weight_total + weight_part
        return (total, weight_total)

    totals, slab_weights = lax.map(pull_slab, slab_numbers)
    grad_features = totals.reshape(share_rows, 9, channels) + cotangent_share.astype(jnp.float32)
    weight_every = lax.psum(jnp.sum(slab_weights, axis=0), ("box", "path"))
    group_paths = PATHS // lax.axis_size("path")
    weight_total = lax.dynamic_slice_in_dim(weight_every, group * group_paths, group_paths, 0)
    return (grad_features, weight_total / math.sqrt(local_rows * lax.axis_size("box")))


def solution(mesh):
    placed = (
        P("box", None, None),
        P(None, "box"),
        P("box", None, None),
        P("path", None, None),
        P("box", None),
        P("box", None),
    )
    return jax.shard_map(
        on_device,
        mesh=mesh,
        in_specs=placed,
        out_specs=(P(("box", "path"), None, None), P("path", None, None)),
        check_vma=False,
    )
```

profile of v0, /device:TPU:0, one launch (start us, length us, event | category | flops | bytes accessed | tf_op | source)
XLA Modules:
  0.0 147.7 jit_solution(1303785314537078605)
XLA Ops:
  0.6 0.8 reshape.2374
  2.6 4.9 %collective-permute-start = (f32[1,3,64]{2,1,0:T(4,128)S(1)}, f32[1,3,64]{2,1,0:T(4,128)S(1)}, u32[]{:S(2)}, u32[]{:S(2)}) collective-permute-start(f32[1,3,64]{2,1,0:T(4,128)S(1)} %get-tuple-element.590), channel_id=1, source_target_pairs={{0,4},{4,8},{8,12},{12,16},{16,20},{20,24},{24,28},{1,5},{5,9},{9,... | collective-permute-start | bytes 2312 | tf_op jit(solution)/shard_map/ppermute | solution.py:51
  7.5 1.3 collective-permute-start.1
  8.8 1.7 %gather_fusion.1 = bf16[2,64,9,128]{3,1,2,0:T(8,128)(2,1)S(1)} fusion(f32[2,64,9,128]{3,1,0,2:T(8,128)} %bitcast.899, s32[1024]{0:T(1024)S(1)} %pad_clamp_fusion), kind=kCustom, calls=%fused_computation.1 | custom fusion | bytes 589832 | tf_op jit(solution)/shard_map/gather | solution.py:164
  11.3 5.2 %collective-permute-start.2 = (bf16[1,64,9,128]{3,1,2,0:T(8,128)(2,1)}, bf16[1,64,9,128]{3,1,2,0:T(8,128)(2,1)}, u32[]{:S(2)}, u32[]{:S(2)}) collective-permute-start(bf16[1,64,9,128]{3,1,2,0:T(8,128)(2,1)} %get-tuple-element.509), channel_id=1, source_target_pairs={{0,4},{4,8},{8,12},{12,16},{16,20},{20,24},{24,28},{1,5},{5,9},{9,... | collective-permute-start | bytes 442376 | tf_op jit(solution)/shard_map/ppermute | solution.py:51
  16.5 1.3 collective-permute-start.3
  20.0 5.2 %all_gather.6 = f32[8,8,128]{2,1,0:T(8,128)S(1)} all-gather(f32[2,8,128]{2,1,0:T(8,128)S(1)} %copy-done.55), channel_id=1, replica_groups=mesh['box'=8,'path'=4] {'path'}, dimensions={0}, use_global_device_ids=true | all-gather | bytes 40960 | tf_op jit(solution)/shard_map/all_gather | solution.py:175
  26.4 1.6 %dynamic-slice_convert_fusion = f32[32,9,128]{2,0,1:T(8,128)} fusion(bf16[128,9,128]{2,0,1:T(8,128)(2,1)} %param.8, s32[]{:T(128)S(6)} %select_n.212), kind=kLoop, calls=%fused_computation.489 | loop fusion | flops 36864 | bytes 221188 | tf_op jit(solution)/shard_map/convert_element_type | solution.py:146
  33.4 0.8 fusion.384
  35.3 0.8 fusion.386
  42.8 0.8 copy-done.33
  43.7 1.8 %concatenate.157 = bf16[256,320]{1,0:T(8,128)(2,1)} concatenate(bf16[256,64]{1,0:T(8,128)(2,1)} %bitcast.946, bf16[256,64]{1,0:T(8,128)(2,1)} %bitcast.945, bf16[256,64]{1,0:T(8,128)(2,1)} %bitcast.944, bf16[256,64]{1,0:T(8,128)(2,1)} %bitcast.943, bf16[256,64]{1,0:T(8,128)(2,1)} %bitcast.942), dimensions={1} | concatenate | bytes 327680 | tf_op jit(solution)/shard_map/while/body/eval_jaxpr/concatenate | solution.py:109
  45.4 1.8 %concatenate.167 = bf16[256,320]{1,0:T(8,128)(2,1)} concatenate(bf16[256,64]{1,0:T(8,128)(2,1)} %bitcast.941, bf16[256,64]{1,0:T(8,128)(2,1)} %bitcast.940, bf16[256,64]{1,0:T(8,128)(2,1)} %bitcast.939, bf16[256,64]{1,0:T(8,128)(2,1)} %bitcast.938, bf16[256,64]{1,0:T(8,128)(2,1)} %bitcast.937), dimensions={1} | concatenate | bytes 327680 | tf_op jit(solution)/shard_map/while/body/eval_jaxpr/concatenate | solution.py:109
  47.2 1.8 %concatenate.147 = bf16[256,320]{1,0:T(8,128)(2,1)} concatenate(bf16[256,64]{1,0:T(8,128)(2,1)} %bitcast.936, bf16[256,64]{1,0:T(8,128)(2,1)} %bitcast.935, bf16[256,64]{1,0:T(8,128)(2,1)} %bitcast.934, bf16[256,64]{1,0:T(8,128)(2,1)} %bitcast.933, bf16[256,64]{1,0:T(8,128)(2,1)} %bitcast.932), dimensions={1} | concatenate | bytes 327680 | tf_op jit(solution)/shard_map/while/body/eval_jaxpr/concatenate | solution.py:109
  49.0 0.8 bitcast_negate_fusion.5
  49.8 1.1 pad_maximum_fusion
  51.1 0.9 copy-done.2
  65.7 6.0 %all_gather.7 = bf16[128,9,128]{2,0,1:T(8,128)(2,1)S(1)} all-gather(bf16[32,9,128]{2,0,1:T(8,128)(2,1)S(1)} %pad_maximum_fusion.1), channel_id=1, replica_groups=mesh['box'=8,'path'=4] {'path'}, dimensions={0}, use_global_device_ids=true | all-gather | bytes 368640 | tf_op jit(solution)/shard_map/all_gather | solution.py:200
  72.5 4.6 %collective-permute-start.4 = (bf16[1,64,9,128]{3,1,2,0:T(8,128)(2,1)S(1)}, bf16[1,64,9,128]{3,1,2,0:T(8,128)(2,1)S(1)}, u32[]{:S(2)}, u32[]{:S(2)}) collective-permute-start(bf16[1,64,9,128]{3,1,2,0:T(8,128)(2,1)S(1)} %get-tuple-element.508), channel_id=1, source_target_pairs={{0,4},{4,8},{8,12},{12,16},{16,20},{20,24},{24,28},{1,5},{5,9},{9,... | collective-permute-start | bytes 442376 | tf_op jit(solution)/shard_map/ppermute | solution.py:51
  77.1 1.5 collective-permute-start.5
  78.6 2.1 %collective-permute-done.4 = bf16[1,64,9,128]{3,1,2,0:T(8,128)(2,1)S(1)} collective-permute-done((bf16[1,64,9,128]{3,1,2,0:T(8,128)(2,1)S(1)}, bf16[1,64,9,128]{3,1,2,0:T(8,128)(2,1)S(1)}, u32[]{:S(2)}, u32[]{:S(2)}) %collective-permute-start.4) | collective-permute-done | bytes 147488 | tf_op jit(solution)/shard_map/ppermute | solution.py:51
  80.7 5.1 %collective-permute-done.5 = bf16[1,64,9,128]{3,1,2,0:T(8,128)(2,1)S(1)} collective-permute-done((bf16[1,64,9,128]{3,1,2,0:T(8,128)(2,1)S(1)}, bf16[1,64,9,128]{3,1,2,0:T(8,128)(2,1)S(1)}, u32[]{:S(2)}, u32[]{:S(2)}) %collective-permute-start.5) | collective-permute-done | bytes 147488 | tf_op jit(solution)/shard_map/ppermute | solution.py:53
  103.4 41.7 %psum.7 = f32[8,8,128]{2,1,0:T(8,128)S(1)} all-reduce(f32[8,8,128]{2,1,0:T(8,128)S(1)} %add_add_fusion.2), channel_id=1, replica_groups=mesh['box'=8,'path'=4] {'box','path'}, use_global_device_ids=true, to_apply=%region_259.260 | all-reduce | flops 8192 | bytes 65536 | tf_op jit(solution)/shard_map/psum | solution.py:224
  146.1 1.6 %add_add_fusion = f32[32,9,128]{2,0,1:T(8,128)} fusion(f32[32,9,128]{2,0,1:T(8,128)S(1)} %constant_dynamic-update-slice_fusion.104, f32[32,9,128]{2,0,1:T(8,128)S(1)} %constant_dynamic-update-slice_fusion.72, f32[32,9,128]{2,0,1:T(8,128)S(1)} %constant_dynamic-update-slice_fusion.88, bf16[128,9,128]{2,0,1:T(8,128)(2,1)} %param.8, s32[]{:T(128)S(6)} %select_n.212), kind=kLoop, calls=%fused_computation.252 | loop fusion | flops 147456 | bytes 663556 | tf_op jit(solution)/shard_map/add | solution.py:223
  (465 shorter events, 43.7 us)
Async XLA Ops:
  2.1 9.2 %copy-start.56 = (s32[1024]{0:T(1024)}, s32[1024]{0:T(1024)S(1)}, u32[]{:S(2)}) copy-start(s32[1024]{0:T(1024)S(1)} %pad_clamp_fusion) | copy-start | bytes 12292
  2.6 29.8 %collective-permute-start = (f32[1,3,64]{2,1,0:T(4,128)S(1)}, f32[1,3,64]{2,1,0:T(4,128)S(1)}, u32[]{:S(2)}, u32[]{:S(2)}) collective-permute-start(f32[1,3,64]{2,1,0:T(4,128)S(1)} %get-tuple-element.590), channel_id=1, source_target_pairs={{0,4},{4,8},{8,12},{12,16},{16,20},{20,24},{24,28},{1,5},{5,9},{9,... | collective-permute-start | bytes 2312 | tf_op jit(solution)/shard_map/ppermute | solution.py:51
  7.5 24.9 %collective-permute-start.1 = (f32[1,3,64]{2,1,0:T(4,128)S(1)}, f32[1,3,64]{2,1,0:T(4,128)S(1)}, u32[]{:S(2)}, u32[]{:S(2)}) collective-permute-start(f32[1,3,64]{2,1,0:T(4,128)S(1)} %get-tuple-element.591), channel_id=1, source_target_pairs={{4,0},{8,4},{12,8},{16,12},{20,16},{24,20},{28,24},{5,1},{9,5},{13... | collective-permute-start | bytes 2312 | tf_op jit(solution)/shard_map/ppermute | solution.py:53
  10.5 7.5 %copy-start = (f32[128,9,128]{2,0,1:T(8,128)S(1)}, f32[128,9,128]{2,0,1:T(8,128)}, u32[]{:S(2)}) copy-start(f32[128,9,128]{2,0,1:T(8,128)} %param.6) | copy-start | bytes 1769476
  10.5 7.5 %copy-start.57 = (s32[2,3]{1,0:T(2,128)S(1)}, s32[2,3]{1,0:T(2,128)}, u32[]{:S(2)}) copy-start(s32[2,3]{1,0:T(2,128)} %param.10) | copy-start | bytes 76
  10.5 9.5 %copy-start.55 = (f32[2,8,128]{2,1,0:T(8,128)S(1)}, f32[2,8,128]{2,1,0:T(8,128)}, u32[]{:S(2)}) copy-start(f32[2,8,128]{2,1,0:T(8,128)} %param.9) | copy-start | bytes 24580
  11.3 38.5 %collective-permute-start.2 = (bf16[1,64,9,128]{3,1,2,0:T(8,128)(2,1)}, bf16[1,64,9,128]{3,1,2,0:T(8,128)(2,1)}, u32[]{:S(2)}, u32[]{:S(2)}) collective-permute-start(bf16[1,64,9,128]{3,1,2,0:T(8,128)(2,1)} %get-tuple-element.509), channel_id=1, source_target_pairs={{0,4},{4,8},{8,12},{12,16},{16,20},{20,24},{24,28},{1,5},{5,9},{9,... | collective-permute-start | bytes 442376 | tf_op jit(solution)/shard_map/ppermute | solution.py:51
  16.5 33.4 %collective-permute-start.3 = (bf16[1,64,9,128]{3,1,2,0:T(8,128)(2,1)}, bf16[1,64,9,128]{3,1,2,0:T(8,128)(2,1)}, u32[]{:S(2)}, u32[]{:S(2)}) collective-permute-start(bf16[1,64,9,128]{3,1,2,0:T(8,128)(2,1)} %get-tuple-element.510), channel_id=1, source_target_pairs={{4,0},{8,4},{12,8},{16,12},{20,16},{24,20},{28,24},{5,1},{9,5},{13... | collective-permute-start | bytes 442376 | tf_op jit(solution)/shard_map/ppermute | solution.py:53
  34.1 2.0 %copy-start.9 = (bf16[1,8,32,64]{3,2,1,0:T(8,128)(2,1)}, bf16[1,8,32,64]{3,2,1,0:T(8,128)(2,1)S(1)}, u32[]{:S(2)}) copy-start(bf16[1,8,32,64]{3,2,1,0:T(8,128)(2,1)S(1)} %get-tuple-element.487) | copy-start | bytes 98308
  34.1 5.9 %copy-start.7 = (bf16[1,8,32,64]{3,2,1,0:T(8,128)(2,1)}, bf16[1,8,32,64]{3,2,1,0:T(8,128)(2,1)S(1)}, u32[]{:S(2)}) copy-start(bf16[1,8,32,64]{3,2,1,0:T(8,128)(2,1)S(1)} %get-tuple-element.480) | copy-start | bytes 98308
  34.1 6.5 %copy-start.11 = (bf16[1,8,32,64]{3,2,1,0:T(8,128)(2,1)}, bf16[1,8,32,64]{3,2,1,0:T(8,128)(2,1)S(1)}, u32[]{:S(2)}) copy-start(bf16[1,8,32,64]{3,2,1,0:T(8,128)(2,1)S(1)} %get-tuple-element.486) | copy-start | bytes 98308
  35.1 1.7 %copy-start.17 = (bf16[1,8,32,64]{3,2,1,0:T(8,128)(2,1)}, bf16[1,8,32,64]{3,2,1,0:T(8,128)(2,1)S(1)}, u32[]{:S(2)}) copy-start(bf16[1,8,32,64]{3,2,1,0:T(8,128)(2,1)S(1)} %get-tuple-element.488) | copy-start | bytes 98308
  35.1 2.3 %copy-start.15 = (bf16[1,8,32,64]{3,2,1,0:T(8,128)(2,1)}, bf16[1,8,32,64]{3,2,1,0:T(8,128)(2,1)S(1)}, u32[]{:S(2)}) copy-start(bf16[1,8,32,64]{3,2,1,0:T(8,128)(2,1)S(1)} %get-tuple-element.494) | copy-start | bytes 98308
  35.1 3.0 %copy-start.19 = (bf16[1,8,32,64]{3,2,1,0:T(8,128)(2,1)}, bf16[1,8,32,64]{3,2,1,0:T(8,128)(2,1)S(1)}, u32[]{:S(2)}) copy-start(bf16[1,8,32,64]{3,2,1,0:T(8,128)(2,1)S(1)} %get-tuple-element.495) | copy-start | bytes 98308
  35.3 1.5 %copy-start.1 = (bf16[9,8,32,64]{3,2,1,0:T(8,128)(2,1)}, bf16[9,8,32,64]{3,2,1,0:T(8,128)(2,1)S(1)}, u32[]{:S(2)}) copy-start(bf16[9,8,32,64]{3,2,1,0:T(8,128)(2,1)S(1)} %multiply_convert_fusion.3) | copy-start | bytes 884740
  36.1 5.4 %copy-start.13 = (bf16[1,8,32,64]{3,2,1,0:T(8,128)(2,1)}, bf16[1,8,32,64]{3,2,1,0:T(8,128)(2,1)S(1)}, u32[]{:S(2)}) copy-start(bf16[1,8,32,64]{3,2,1,0:T(8,128)(2,1)S(1)} %get-tuple-element.503) | copy-start | bytes 98308
  36.1 5.4 %copy-start.21 = (bf16[1,8,32,64]{3,2,1,0:T(8,128)(2,1)}, bf16[1,8,32,64]{3,2,1,0:T(8,128)(2,1)S(1)}, u32[]{:S(2)}) copy-start(bf16[1,8,32,64]{3,2,1,0:T(8,128)(2,1)S(1)} %get-tuple-element.502) | copy-start | bytes 98308
  50.9 1.3 copy-start.39
  51.0 1.9 %copy-start.49 = (f32[8,128]{1,0:T(8,128)S(1)}, f32[8,128]{1,0:T(8,128)}, u32[]{:S(2)}) copy-start(f32[8,128]{1,0:T(8,128)} %get-tuple-element.532) | copy-start | bytes 12292
  52.0 1.2 copy-start.37
  53.2 1.2 copy-start.53
  60.2 1.1 copy-start.14
  72.5 8.2 %collective-permute-start.4 = (bf16[1,64,9,128]{3,1,2,0:T(8,128)(2,1)S(1)}, bf16[1,64,9,128]{3,1,2,0:T(8,128)(2,1)S(1)}, u32[]{:S(2)}, u32[]{:S(2)}) collective-permute-start(bf16[1,64,9,128]{3,1,2,0:T(8,128)(2,1)S(1)} %get-tuple-element.508), channel_id=1, source_target_pairs={{0,4},{4,8},{8,12},{12,16},{16,20},{20,24},{24,28},{1,5},{5,9},{9,... | collective-permute-start | bytes 442376 | tf_op jit(solution)/shard_map/ppermute | solution.py:51
  77.1 8.7 %collective-permute-start.5 = (bf16[1,64,9,128]{3,1,2,0:T(8,128)(2,1)S(1)}, bf16[1,64,9,128]{3,1,2,0:T(8,128)(2,1)S(1)}, u32[]{:S(2)}, u32[]{:S(2)}) collective-permute-start(bf16[1,64,9,128]{3,1,2,0:T(8,128)(2,1)S(1)} %get-tuple-element.507), channel_id=1, source_target_pairs={{4,0},{8,4},{12,8},{16,12},{20,16},{24,20},{28,24},{5,1},{9,5},{13... | collective-permute-start | bytes 442376 | tf_op jit(solution)/shard_map/ppermute | solution.py:53
  (40 other events, 34.2 us)
where the time goes:
time: 149 us; the launch traced here: 148 us
  blocking collectives  53 us (36%)
  matrix products  25 us (17%)
  local copies, waits for them, and re-layouts  20.3 us (14%)
  starting transfers between devices  18.7 us (13%)
  other arithmetic  14.5 us (10%)
  between operations  9.16 us (6%)
  waiting for transfers between devices  7.16 us (5%)
    psum x1, blocking collectives, on_device(): weight_every = lax.psum(jnp.sum(slab_weights, axis=0), ('box', 'path'))  41.7 us
    ppermute x3, starting transfers between devices, with_halo(): lax.ppermute(tail, axis, [(i, (i + 1) % count) for i in range(ends)])  14.6 us
    dot_general x93, matrix products, transpose_terms(): lax.dot_general(edge_table[harmonic], cotangent_rows[:, output, :], (((1,...  14.4 us
    dot_general x66, matrix products, forward_terms(): jnp.dot(jnp.concatenate(pieces, axis=1), jnp.concatenate(stacked, axis=0)...  10.6 us
    all_gather x1, blocking collectives, on_device(): message_cotangent = lax.all_gather(gate_rows, 'path', axis=0, tiled=True)  6.04 us
    unnamed x139, local copies, waits for them, and re-layouts  6.02 us
    neg x9, other arithmetic, forward_terms(): signed = edge_table[harmonic] if factor > 0 else -edge_table[harmonic]  6.01 us
    concatenate x3, local copies, waits for them, and re-layouts, forward_terms(): jnp.concatenate(pieces, axis=1)  5.3 us
  transfers between devices with their start and end apart: 6, of which 2 were waited for; matrix products, arithmetic and copies ran while one was open for 15% of the time, Pallas kernels for 0%

commit v1 on v0

--- a/solution.py
+++ b/solution.py
@@ -221,7 +221,7 @@
 
     totals, slab_weights = lax.map(pull_slab, slab_numbers)
     grad_features = totals.reshape(share_rows, 9, channels) + cotangent_share.astype(jnp.float32)
-    weight_every = lax.psum(jnp.sum(slab_weights, axis=0), ("box", "path"))
+    weight_every = lax.psum(lax.psum(jnp.sum(slab_weights, axis=0), "box"), "path")
     group_paths = PATHS // lax.axis_size("path")
     weight_total = lax.dynamic_slice_in_dim(weight_every, group * group_paths, group_paths, 0)
     return (grad_features, weight_total / math.sqrt(local_rows * lax.axis_size("box")))

time: 149 us -> 154 us (1.034)
  blocking collectives: 53 us -> 58 us
    psum x1 -> x2, blocking collectives: 41.7 us -> 46.8 us  [the longest x1 36.6 us: on_device(): lax.psum(jnp.sum(slab_weights, axis=0), 'box')]
  transfers between devices with their start and end apart: 6 -> 6, of which waited for: 2 -> 2; matrix products, arithmetic and copies ran while one was open for 15% -> 14% of each run, Pallas kernels for 0% -> 0%
where the time goes in v1:
time: 154 us; the launch traced here: 153 us
  blocking collectives  58 us (38%)
  matrix products  25 us (16%)
  local copies, waits for them, and re-layouts  20.3 us (13%)
  starting transfers between devices  18.7 us (12%)
  other arithmetic  14.5 us (9%)
  between operations  9.16 us (6%)
  waiting for transfers between devices  7.16 us (5%)
    psum x1, blocking collectives, on_device(): lax.psum(jnp.sum(slab_weights, axis=0), 'box')  36.6 us
    ppermute x3, starting transfers between devices, with_halo(): lax.ppermute(tail, axis, [(i, (i + 1) % count) for i in range(ends)])  14.6 us
    dot_general x93, matrix products, transpose_terms(): lax.dot_general(edge_table[harmonic], cotangent_rows[:, output, :], (((1,...  14.4 us
    dot_general x66, matrix products, forward_terms(): jnp.dot(jnp.concatenate(pieces, axis=1), jnp.concatenate(stacked, axis=0)...  10.6 us
    psum x1, blocking collectives, on_device(): lax.psum(lax.psum(jnp.sum(slab_weights, axis=0), 'box'), 'path')  10.3 us
    all_gather x1, blocking collectives, on_device(): message_cotangent = lax.all_gather(gate_rows, 'path', axis=0, tiled=True)  6.04 us
    unnamed x139, local copies, waits for them, and re-layouts  6.02 us
    neg x9, other arithmetic, forward_terms(): signed = edge_table[harmonic] if factor > 0 else -edge_table[harmonic]  6.01 us
  transfers between devices with their start and end apart: 6, of which 2 were waited for; matrix products, arithmetic and copies ran while one was open for 14% of the time, Pallas kernels for 0%

profile of v1, /device:TPU:0, one launch (start us, length us, event | category | flops | bytes accessed | tf_op | source)
XLA Modules:
  0.0 152.8 jit_solution(3944988234929174868)
XLA Ops:
  0.6 0.8 reshape.2374
  2.6 4.9 %collective-permute-start = (f32[1,3,64]{2,1,0:T(4,128)S(1)}, f32[1,3,64]{2,1,0:T(4,128)S(1)}, u32[]{:S(2)}, u32[]{:S(2)}) collective-permute-start(f32[1,3,64]{2,1,0:T(4,128)S(1)} %get-tuple-element.590), channel_id=1, source_target_pairs={{0,4},{4,8},{8,12},{12,16},{16,20},{20,24},{24,28},{1,5},{5,9},{9,... | collective-permute-start | bytes 2312 | tf_op jit(solution)/shard_map/ppermute | solution.py:51
  7.5 1.3 collective-permute-start.1
  8.8 1.7 %gather_fusion.1 = bf16[2,64,9,128]{3,1,2,0:T(8,128)(2,1)S(1)} fusion(f32[2,64,9,128]{3,1,0,2:T(8,128)} %bitcast.899, s32[1024]{0:T(1024)S(1)} %pad_clamp_fusion), kind=kCustom, calls=%fused_computation.1 | custom fusion | bytes 589832 | tf_op jit(solution)/shard_map/gather | solution.py:164
  11.3 5.2 %collective-permute-start.2 = (bf16[1,64,9,128]{3,1,2,0:T(8,128)(2,1)}, bf16[1,64,9,128]{3,1,2,0:T(8,128)(2,1)}, u32[]{:S(2)}, u32[]{:S(2)}) collective-permute-start(bf16[1,64,9,128]{3,1,2,0:T(8,128)(2,1)} %get-tuple-element.509), channel_id=1, source_target_pairs={{0,4},{4,8},{8,12},{12,16},{16,20},{20,24},{24,28},{1,5},{5,9},{9,... | collective-permute-start | bytes 442376 | tf_op jit(solution)/shard_map/ppermute | solution.py:51
  16.5 1.3 collective-permute-start.3
  20.0 5.2 %all_gather.6 = f32[8,8,128]{2,1,0:T(8,128)S(1)} all-gather(f32[2,8,128]{2,1,0:T(8,128)S(1)} %copy-done.55), channel_id=1, replica_groups=mesh['box'=8,'path'=4] {'path'}, dimensions={0}, use_global_device_ids=true | all-gather | bytes 40960 | tf_op jit(solution)/shard_map/all_gather | solution.py:175
  26.4 1.6 %dynamic-slice_convert_fusion = f32[32,9,128]{2,0,1:T(8,128)} fusion(bf16[128,9,128]{2,0,1:T(8,128)(2,1)} %param.8, s32[]{:T(128)S(6)} %select_n.212), kind=kLoop, calls=%fused_computation.489 | loop fusion | flops 36864 | bytes 221188 | tf_op jit(solution)/shard_map/convert_element_type | solution.py:146
  35.3 0.8 fusion.386
  42.8 0.8 copy-done.33
  43.7 1.8 %concatenate.157 = bf16[256,320]{1,0:T(8,128)(2,1)} concatenate(bf16[256,64]{1,0:T(8,128)(2,1)} %bitcast.946, bf16[256,64]{1,0:T(8,128)(2,1)} %bitcast.945, bf16[256,64]{1,0:T(8,128)(2,1)} %bitcast.944, bf16[256,64]{1,0:T(8,128)(2,1)} %bitcast.943, bf16[256,64]{1,0:T(8,128)(2,1)} %bitcast.942), dimensions={1} | concatenate | bytes 327680 | tf_op jit(solution)/shard_map/while/body/eval_jaxpr/concatenate | solution.py:109
  45.4 1.8 %concatenate.167 = bf16[256,320]{1,0:T(8,128)(2,1)} concatenate(bf16[256,64]{1,0:T(8,128)(2,1)} %bitcast.941, bf16[256,64]{1,0:T(8,128)(2,1)} %bitcast.940, bf16[256,64]{1,0:T(8,128)(2,1)} %bitcast.939, bf16[256,64]{1,0:T(8,128)(2,1)} %bitcast.938, bf16[256,64]{1,0:T(8,128)(2,1)} %bitcast.937), dimensions={1} | concatenate | bytes 327680 | tf_op jit(solution)/shard_map/while/body/eval_jaxpr/concatenate | solution.py:109
  47.2 1.8 %concatenate.147 = bf16[256,320]{1,0:T(8,128)(2,1)} concatenate(bf16[256,64]{1,0:T(8,128)(2,1)} %bitcast.936, bf16[256,64]{1,0:T(8,128)(2,1)} %bitcast.935, bf16[256,64]{1,0:T(8,128)(2,1)} %bitcast.934, bf16[256,64]{1,0:T(8,128)(2,1)} %bitcast.933, bf16[256,64]{1,0:T(8,128)(2,1)} %bitcast.932), dimensions={1} | concatenate | bytes 327680 | tf_op jit(solution)/shard_map/while/body/eval_jaxpr/concatenate | solution.py:109
  49.0 0.8 bitcast_negate_fusion.5
  49.8 1.1 pad_maximum_fusion
  51.1 0.9 copy-done.2
  65.7 6.0 %all_gather.7 = bf16[128,9,128]{2,0,1:T(8,128)(2,1)S(1)} all-gather(bf16[32,9,128]{2,0,1:T(8,128)(2,1)S(1)} %pad_maximum_fusion.1), channel_id=1, replica_groups=mesh['box'=8,'path'=4] {'path'}, dimensions={0}, use_global_device_ids=true | all-gather | bytes 368640 | tf_op jit(solution)/shard_map/all_gather | solution.py:200
  72.5 4.6 %collective-permute-start.4 = (bf16[1,64,9,128]{3,1,2,0:T(8,128)(2,1)S(1)}, bf16[1,64,9,128]{3,1,2,0:T(8,128)(2,1)S(1)}, u32[]{:S(2)}, u32[]{:S(2)}) collective-permute-start(bf16[1,64,9,128]{3,1,2,0:T(8,128)(2,1)S(1)} %get-tuple-element.508), channel_id=1, source_target_pairs={{0,4},{4,8},{8,12},{12,16},{16,20},{20,24},{24,28},{1,5},{5,9},{9,... | collective-permute-start | bytes 442376 | tf_op jit(solution)/shard_map/ppermute | solution.py:51
  77.1 1.5 collective-permute-start.5
  78.6 2.1 %collective-permute-done.4 = bf16[1,64,9,128]{3,1,2,0:T(8,128)(2,1)S(1)} collective-permute-done((bf16[1,64,9,128]{3,1,2,0:T(8,128)(2,1)S(1)}, bf16[1,64,9,128]{3,1,2,0:T(8,128)(2,1)S(1)}, u32[]{:S(2)}, u32[]{:S(2)}) %collective-permute-start.4) | collective-permute-done | bytes 147488 | tf_op jit(solution)/shard_map/ppermute | solution.py:51
  80.7 5.1 %collective-permute-done.5 = bf16[1,64,9,128]{3,1,2,0:T(8,128)(2,1)S(1)} collective-permute-done((bf16[1,64,9,128]{3,1,2,0:T(8,128)(2,1)S(1)}, bf16[1,64,9,128]{3,1,2,0:T(8,128)(2,1)S(1)}, u32[]{:S(2)}, u32[]{:S(2)}) %collective-permute-start.5) | collective-permute-done | bytes 147488 | tf_op jit(solution)/shard_map/ppermute | solution.py:53
  103.4 36.6 %psum.14 = f32[8,8,128]{2,1,0:T(8,128)S(1)} all-reduce(f32[8,8,128]{2,1,0:T(8,128)S(1)} %add_add_fusion.2), channel_id=1, replica_groups=mesh['box'=8,'path'=4] {'box'}, use_global_device_ids=true, to_apply=%region_259.260 | all-reduce | flops 8192 | bytes 65536 | tf_op jit(solution)/shard_map/psum | solution.py:224
  139.9 10.3 %psum.15 = f32[8,8,128]{2,1,0:T(8,128)S(1)} all-reduce(f32[8,8,128]{2,1,0:T(8,128)S(1)} %psum.14), channel_id=1, replica_groups=mesh['box'=8,'path'=4] {'path'}, use_global_device_ids=true, to_apply=%region_260.261 | all-reduce | flops 8192 | bytes 65536 | tf_op jit(solution)/shard_map/psum | solution.py:224
  151.2 1.6 %add_add_fusion = f32[32,9,128]{2,0,1:T(8,128)} fusion(f32[32,9,128]{2,0,1:T(8,128)S(1)} %constant_dynamic-update-slice_fusion.104, f32[32,9,128]{2,0,1:T(8,128)S(1)} %constant_dynamic-update-slice_fusion.72, f32[32,9,128]{2,0,1:T(8,128)S(1)} %constant_dynamic-update-slice_fusion.88, bf16[128,9,128]{2,0,1:T(8,128)(2,1)} %param.8, s32[]{:T(128)S(6)} %select_n.212), kind=kLoop, calls=%fused_computation.252 | loop fusion | flops 147456 | bytes 663556 | tf_op jit(solution)/shard_map/add | solution.py:223
  (466 shorter events, 44.5 us)
Async XLA Ops:
  2.1 9.2 %copy-start.56 = (s32[1024]{0:T(1024)}, s32[1024]{0:T(1024)S(1)}, u32[]{:S(2)}) copy-start(s32[1024]{0:T(1024)S(1)} %pad_clamp_fusion) | copy-start | bytes 12292
  2.6 29.8 %collective-permute-start = (f32[1,3,64]{2,1,0:T(4,128)S(1)}, f32[1,3,64]{2,1,0:T(4,128)S(1)}, u32[]{:S(2)}, u32[]{:S(2)}) collective-permute-start(f32[1,3,64]{2,1,0:T(4,128)S(1)} %get-tuple-element.590), channel_id=1, source_target_pairs={{0,4},{4,8},{8,12},{12,16},{16,20},{20,24},{24,28},{1,5},{5,9},{9,... | collective-permute-start | bytes 2312 | tf_op jit(solution)/shard_map/ppermute | solution.py:51
  7.5 24.9 %collective-permute-start.1 = (f32[1,3,64]{2,1,0:T(4,128)S(1)}, f32[1,3,64]{2,1,0:T(4,128)S(1)}, u32[]{:S(2)}, u32[]{:S(2)}) collective-permute-start(f32[1,3,64]{2,1,0:T(4,128)S(1)} %get-tuple-element.591), channel_id=1, source_target_pairs={{4,0},{8,4},{12,8},{16,12},{20,16},{24,20},{28,24},{5,1},{9,5},{13... | collective-permute-start | bytes 2312 | tf_op jit(solution)/shard_map/ppermute | solution.py:53
  10.5 7.5 %copy-start = (f32[128,9,128]{2,0,1:T(8,128)S(1)}, f32[128,9,128]{2,0,1:T(8,128)}, u32[]{:S(2)}) copy-start(f32[128,9,128]{2,0,1:T(8,128)} %param.6) | copy-start | bytes 1769476
  10.5 7.5 %copy-start.57 = (s32[2,3]{1,0:T(2,128)S(1)}, s32[2,3]{1,0:T(2,128)}, u32[]{:S(2)}) copy-start(s32[2,3]{1,0:T(2,128)} %param.10) | copy-start | bytes 76
  10.5 9.5 %copy-start.55 = (f32[2,8,128]{2,1,0:T(8,128)S(1)}, f32[2,8,128]{2,1,0:T(8,128)}, u32[]{:S(2)}) copy-start(f32[2,8,128]{2,1,0:T(8,128)} %param.9) | copy-start | bytes 24580
  11.3 38.5 %collective-permute-start.2 = (bf16[1,64,9,128]{3,1,2,0:T(8,128)(2,1)}, bf16[1,64,9,128]{3,1,2,0:T(8,128)(2,1)}, u32[]{:S(2)}, u32[]{:S(2)}) collective-permute-start(bf16[1,64,9,128]{3,1,2,0:T(8,128)(2,1)} %get-tuple-element.509), channel_id=1, source_target_pairs={{0,4},{4,8},{8,12},{12,16},{16,20},{20,24},{24,28},{1,5},{5,9},{9,... | collective-permute-start | bytes 442376 | tf_op jit(solution)/shard_map/ppermute | solution.py:51
  16.5 33.4 %collective-permute-start.3 = (bf16[1,64,9,128]{3,1,2,0:T(8,128)(2,1)}, bf16[1,64,9,128]{3,1,2,0:T(8,128)(2,1)}, u32[]{:S(2)}, u32[]{:S(2)}) collective-permute-start(bf16[1,64,9,128]{3,1,2,0:T(8,128)(2,1)} %get-tuple-element.510), channel_id=1, source_target_pairs={{4,0},{8,4},{12,8},{16,12},{20,16},{24,20},{28,24},{5,1},{9,5},{13... | collective-permute-start | bytes 442376 | tf_op jit(solution)/shard_map/ppermute | solution.py:53
  34.1 2.0 %copy-start.9 = (bf16[1,8,32,64]{3,2,1,0:T(8,128)(2,1)}, bf16[1,8,32,64]{3,2,1,0:T(8,128)(2,1)S(1)}, u32[]{:S(2)}) copy-start(bf16[1,8,32,64]{3,2,1,0:T(8,128)(2,1)S(1)} %get-tuple-element.487) | copy-start | bytes 98308
  34.1 5.9 %copy-start.7 = (bf16[1,8,32,64]{3,2,1,0:T(8,128)(2,1)}, bf16[1,8,32,64]{3,2,1,0:T(8,128)(2,1)S(1)}, u32[]{:S(2)}) copy-start(bf16[1,8,32,64]{3,2,1,0:T(8,128)(2,1)S(1)} %get-tuple-element.480) | copy-start | bytes 98308
  34.1 6.5 %copy-start.11 = (bf16[1,8,32,64]{3,2,1,0:T(8,128)(2,1)}, bf16[1,8,32,64]{3,2,1,0:T(8,128)(2,1)S(1)}, u32[]{:S(2)}) copy-start(bf16[1,8,32,64]{3,2,1,0:T(8,128)(2,1)S(1)} %get-tuple-element.486) | copy-start | bytes 98308
  35.1 1.7 %copy-start.17 = (bf16[1,8,32,64]{3,2,1,0:T(8,128)(2,1)}, bf16[1,8,32,64]{3,2,1,0:T(8,128)(2,1)S(1)}, u32[]{:S(2)}) copy-start(bf16[1,8,32,64]{3,2,1,0:T(8,128)(2,1)S(1)} %get-tuple-element.488) | copy-start | bytes 98308
  35.1 2.3 %copy-start.15 = (bf16[1,8,32,64]{3,2,1,0:T(8,128)(2,1)}, bf16[1,8,32,64]{3,2,1,0:T(8,128)(2,1)S(1)}, u32[]{:S(2)}) copy-start(bf16[1,8,32,64]{3,2,1,0:T(8,128)(2,1)S(1)} %get-tuple-element.494) | copy-start | bytes 98308
  35.1 3.0 %copy-start.19 = (bf16[1,8,32,64]{3,2,1,0:T(8,128)(2,1)}, bf16[1,8,32,64]{3,2,1,0:T(8,128)(2,1)S(1)}, u32[]{:S(2)}) copy-start(bf16[1,8,32,64]{3,2,1,0:T(8,128)(2,1)S(1)} %get-tuple-element.495) | copy-start | bytes 98308
  35.3 1.5 copy-start.1
  36.1 5.4 %copy-start.13 = (bf16[1,8,32,64]{3,2,1,0:T(8,128)(2,1)}, bf16[1,8,32,64]{3,2,1,0:T(8,128)(2,1)S(1)}, u32[]{:S(2)}) copy-start(bf16[1,8,32,64]{3,2,1,0:T(8,128)(2,1)S(1)} %get-tuple-element.503) | copy-start | bytes 98308
  36.1 5.4 %copy-start.21 = (bf16[1,8,32,64]{3,2,1,0:T(8,128)(2,1)}, bf16[1,8,32,64]{3,2,1,0:T(8,128)(2,1)S(1)}, u32[]{:S(2)}) copy-start(bf16[1,8,32,64]{3,2,1,0:T(8,128)(2,1)S(1)} %get-tuple-element.502) | copy-start | bytes 98308
  50.9 1.3 copy-start.39
  51.0 1.9 %copy-start.49 = (f32[8,128]{1,0:T(8,128)S(1)}, f32[8,128]{1,0:T(8,128)}, u32[]{:S(2)}) copy-start(f32[8,128]{1,0:T(8,128)} %get-tuple-element.532) | copy-start | bytes 12292
  52.0 1.2 copy-start.37
  53.2 1.2 copy-start.53
  60.2 1.1 copy-start.14
  72.5 8.2 %collective-permute-start.4 = (bf16[1,64,9,128]{3,1,2,0:T(8,128)(2,1)S(1)}, bf16[1,64,9,128]{3,1,2,0:T(8,128)(2,1)S(1)}, u32[]{:S(2)}, u32[]{:S(2)}) collective-permute-start(bf16[1,64,9,128]{3,1,2,0:T(8,128)(2,1)S(1)} %get-tuple-element.508), channel_id=1, source_target_pairs={{0,4},{4,8},{8,12},{12,16},{16,20},{20,24},{24,28},{1,5},{5,9},{9,... | collective-permute-start | bytes 442376 | tf_op jit(solution)/shard_map/ppermute | solution.py:51
  77.1 8.7 %collective-permute-start.5 = (bf16[1,64,9,128]{3,1,2,0:T(8,128)(2,1)S(1)}, bf16[1,64,9,128]{3,1,2,0:T(8,128)(2,1)S(1)}, u32[]{:S(2)}, u32[]{:S(2)}) collective-permute-start(bf16[1,64,9,128]{3,1,2,0:T(8,128)(2,1)S(1)} %get-tuple-element.507), channel_id=1, source_target_pairs={{4,0},{8,4},{12,8},{16,12},{20,16},{24,20},{28,24},{5,1},{9,5},{13... | collective-permute-start | bytes 442376 | tf_op jit(solution)/shard_map/ppermute | solution.py:53
  (40 other events, 34.2 us)
